TPU v7x, 32 devices: a whole 2x2x4 slice. The times are simulated.
32 devices in a mesh: row: 4 (over z), col: 2 (over x), depth: 4 (over y, core).
Axes of the slice: x: 2, y: 2, z: 4, core: 2. Of those that a mesh axis runs over, the one named last changes fastest.
Arguments:
- tokens: bfloat16 [2560, 8192], P(('row', 'depth'), 'col'), may hold values from -6 to 6
- weight: bfloat16 [8192, 4096], P('row', 'col'), may hold values from -0.0625 to 0.0625
- cotangent: bfloat16 [2560, 4096], P(('row', 'depth'), 'col'), may hold values from -6 to 6
- master: float32 [8192, 4096], P(('row', 'depth'), 'col'), may hold values from -0.1 to 0.1
- first_moment: float32 [8192, 4096], P(('row', 'depth'), 'col'), may hold values from -6 to 6
- second_moment: float32 [8192, 4096], P(('row', 'depth'), 'col'), may hold values from 0.1 to 10
Outputs:
- queries: bfloat16 [2560, 4096], P(('row', 'depth'), 'col')
- token_grad: bfloat16 [2560, 8192], P(('row', 'depth'), 'col')
- new_master: float32 [8192, 4096], P(('row', 'depth'), 'col')
- new_first: float32 [8192, 4096], P(('row', 'depth'), 'col')
- new_second: float32 [8192, 4096], P(('row', 'depth'), 'col')
- new_weight: bfloat16 [8192, 4096], P('row', 'col')
All inputs are finite; a program needn't handle non-finite values.
Results may differ from a plain program's by a relative error of at most 0.001.
Values may be sent and summed in bfloat16 or wider, within the bound.
A program may use at most 128 MiB of HBM per device.

v0:
```python
import math
import jax
import jax.numpy as jnp
from jax import lax
from jax.sharding import PartitionSpec as P

beta_one = 0.9
beta_two = 0.95
learn_rate = 0.02
decay_rate = 0.1
adam_eps = 1e-08
bias_one = 1.0 - 0.9**50
bias_two = 1.0 - 0.95**50


def local(tokens, weight, cotangent, master, first_moment, second_moment):
    total_tokens = tokens.shape[0] * lax.axis_size("row") * lax.axis_size("depth")
    grad_scale = 1.0 / math.sqrt(total_tokens)
    full_rows = lax.all_gather(tokens, "col", axis=1, tiled=True)
    full_panel = lax.all_gather(weight, "row", axis=0, tiled=True)
    queries = jnp.dot(full_rows, full_panel, preferred_element_type=jnp.float32).astype(
        jnp.bfloat16
    )
    partial_value = lax.dot_general(
        cotangent, full_panel, (((1,), (1,)), ((), ())), preferred_element_type=jnp.float32
    )
    token_grad = lax.psum_scatter(partial_value, "col", scatter_dimension=1, tiled=True).astype(
        jnp.bfloat16
    )
    token_slab = lax.all_to_all(
        full_rows, ("row", "depth"), split_axis=1, concat_axis=0, tiled=True
    )
    product = lax.dot_general(
        token_slab,
        lax.all_gather(cotangent, ("row", "depth"), axis=0, tiled=True),
        (((0,), (0,)), ((), ())),
        preferred_element_type=jnp.float32,
    )
    grad = product * grad_scale
    new_first = beta_one * first_moment + (1.0 - beta_one) * grad
    new_second = beta_two * second_moment + (1.0 - beta_two) * grad * grad
    step_value = new_first / bias_one / (jnp.sqrt(new_second / bias_two) + adam_eps)
    new_master = master - learn_rate * (step_value + decay_rate * master)
    shard_weight = new_master.astype(jnp.bfloat16)
    new_weight = lax.all_gather(shard_weight, "depth", axis=0, tiled=True)
    return (queries, token_grad, new_master, new_first, new_second, new_weight)


def solution(mesh):
    in_specs = (
        P(("row", "depth"), "col"),
        P("row", "col"),
        P(("row", "depth"), "col"),
        P(("row", "depth"), "col"),
        P(("row", "depth"), "col"),
        P(("row", "depth"), "col"),
    )
    out_specs = (
        P(("row", "depth"), "col"),
        P(("row", "depth"), "col"),
        P(("row", "depth"), "col"),
        P(("row", "depth"), "col"),
        P(("row", "depth"), "col"),
        P("row", "col"),
    )
    return jax.shard_map(local, mesh=mesh, in_specs=in_specs, out_specs=out_specs, check_vma=False)
```

profile of v0, /device:TPU:0, one launch (start us, length us, event | category | flops | bytes accessed | tf_op | source)
XLA Modules:
  0.0 889.6 jit_solution(17956850485688772737)
XLA Ops:
  7.2 0.0 all-gather.5.cloned.1.call-start
  7.2 0.7 all-gather.5.cloned.1.call-update
  7.9 0.0 all-gather.9.cloned.1.call-start
  7.9 0.7 all-gather.9.cloned.1.call-update
  8.6 0.0 all-gather.7.cloned.1.call-start
  8.7 0.7 all-gather.7.cloned.1.call-update
  9.4 0.0 all-gather.11.cloned.1.call-start
  9.4 41.8 %all-gather.5.cloned.1.call-done = bf16[160,8192]{1,0:T(8,128)(2,1)} async-done(((bf16[160,4096]{1,0:T(8,128)(2,1)}), bf16[160,8192]{1,0:T(8,128)(2,1)}) %all-gather.5.cloned.1.call-update) | async-done | bytes 2621456 | tf_op jit(solution)/shard_map/all_gather | solution.py:19
  51.3 2.0 copy.16
  53.3 113.0 %all_to_all.19 = bf16[160,16,512]{2,0,1:T(8,128)(2,1)S(1)} all-to-all(bf16[160,16,512]{2,0,1:T(8,128)(2,1)S(1)} %bitcast.13), channel_id=1, replica_groups=mesh['row'=4,'col'=2,'depth'=4] {'row','depth'}, dimensions={1} | all-to-all | bytes 5242880 | tf_op jit(solution)/shard_map/all_to_all | solution.py:30
  166.3 17.8 %all-gather.9.cloned.1.call-done = bf16[2560,2048]{1,0:T(8,128)(2,1)} async-done(((bf16[160,2048]{1,0:T(8,128)(2,1)}), bf16[2560,2048]{1,0:T(8,128)(2,1)}) %all-gather.9.cloned.1.call-update) | async-done | bytes 10485776 | tf_op jit(solution)/shard_map/all_gather | solution.py:35
  184.1 0.0 copy-start
  184.1 18.9 %fusion = (bf16[512,2048]{1,0:T(8,128)(2,1)}, f32[512,2048]{1,0:T(8,128)}, f32[512,2048]{1,0:T(8,128)}, f32[512,2048]{1,0:T(8,128)}) fusion(f32[512,2048]{1,0:T(8,128)} %param.9, f32[512,2048]{1,0:T(8,128)} %param.10, f32[512,2048]{1,0:T(8,128)} %param.11, bf16[2560,512]{1,0:T(8,128)(2,1)S(1)} %bitcast.15, bf16[2560,2048]{1,0:T(8,128)(2,1)} %all-gather.9.cloned.1.call-done), kind=kOutput, calls=%fused_computation.5 | convolution fusion | flops 5386534912 | bytes 40370176 | tf_op jit(solution)/shard_map/dot_general | solution.py:33
  203.0 0.0 all-gather.11.cloned.1.call-update
  203.0 0.0 reduce-scatter.2.cloned.1.call-start
  203.1 542.1 %all-gather.7.cloned.1.call-done = bf16[8192,2048]{1,0:T(8,128)(2,1)} async-done(((bf16[2048,2048]{1,0:T(8,128)(2,1)}), bf16[8192,2048]{1,0:T(8,128)(2,1)}) %all-gather.7.cloned.1.call-update) | async-done | bytes 33554448 | tf_op jit(solution)/shard_map/all_gather | solution.py:20
  745.2 0.0 copy-done
  745.2 19.8 %fusion.1 = f32[160,8192]{1,0:T(8,128)} fusion(bf16[160,2048]{1,0:T(8,128)(2,1)S(1)} %copy-done, bf16[8192,2048]{1,0:T(8,128)(2,1)} %all-gather.7.cloned.1.call-done), kind=kOutput, calls=%fused_computation.6 | convolution fusion | flops 5368709120 | bytes 39452672 | tf_op jit(solution)/shard_map/dot_general | solution.py:24
  765.0 0.0 copy-start.1
  765.0 0.0 reduce-scatter.2.cloned.1.call-update
  765.1 38.1 %all-gather.11.cloned.1.call-done = bf16[2048,2048]{1,0:T(8,128)(2,1)} async-done(((bf16[512,2048]{1,0:T(8,128)(2,1)}), bf16[2048,2048]{1,0:T(8,128)(2,1)}) %all-gather.11.cloned.1.call-update) | async-done | bytes 8388624 | tf_op jit(solution)/shard_map/all_gather | solution.py:45
  803.1 0.0 copy-done.1
  803.1 15.2 %convolution_convert_fusion = bf16[160,2048]{1,0:T(8,128)(2,1)} fusion(bf16[160,8192]{1,0:T(8,128)(2,1)S(1)} %copy-done.1, bf16[8192,2048]{1,0:T(8,128)(2,1)} %all-gather.7.cloned.1.call-done), kind=kOutput, calls=%fused_computation.4 | convolution fusion | flops 5369036800 | bytes 36831232 | tf_op jit(solution)/shard_map/dot_general | solution.py:21
  818.3 53.3 %reduce-scatter.2.cloned.1.call-done = f32[160,4096]{1,0:T(8,128)} async-done(((f32[160,8192]{1,0:T(8,128)}), f32[160,4096]{1,0:T(8,128)}) %reduce-scatter.2.cloned.1.call-update) | async-done | bytes 2621456 | tf_op jit(solution)/shard_map/reduce_scatter | solution.py:27
  871.6 3.0 convert_element_type.10
  874.6 8.4 copy.18
Async XLA Ops:
  7.2 44.1 %all-gather.5.cloned.1.call-start = ((), (), s32[]{:S(2)}) async-start(), calls=%async_computation.2 | async-start | bytes 3932160 | tf_op jit(solution)/shard_map/all_gather | solution.py:19
  7.9 176.2 %all-gather.9.cloned.1.call-start = ((), (), s32[]{:S(2)}) async-start(), calls=%async_computation.5 | async-start | bytes 11141120 | tf_op jit(solution)/shard_map/all_gather | solution.py:35
  8.6 736.6 %all-gather.7.cloned.1.call-start = ((), (), s32[]{:S(2)}) async-start(), calls=%async_computation.3 | async-start | bytes 41943040 | tf_op jit(solution)/shard_map/all_gather | solution.py:20
  9.4 793.7 %all-gather.11.cloned.1.call-start = ((), (), s32[]{:S(2)}) async-start(), calls=%async_computation.6 | async-start | bytes 10485760 | tf_op jit(solution)/shard_map/all_gather | solution.py:45
  184.1 561.1 %copy-start = (bf16[160,2048]{1,0:T(8,128)(2,1)S(1)}, bf16[160,2048]{1,0:T(8,128)(2,1)}, u32[]{:S(2)}) copy-start(bf16[160,2048]{1,0:T(8,128)(2,1)} %param.8) | copy-start | bytes 1966084
  203.0 668.6 %reduce-scatter.2.cloned.1.call-start = ((), (), s32[]{:S(2)}) async-start(), calls=%async_computation.4 | async-start | bytes 7864320 | tf_op jit(solution)/shard_map/reduce_scatter | solution.py:27
  765.0 38.1 %copy-start.1 = (bf16[160,8192]{1,0:T(8,128)(2,1)S(1)}, bf16[160,8192]{1,0:T(8,128)(2,1)}, u32[]{:S(2)}) copy-start(bf16[160,8192]{1,0:T(8,128)(2,1)} %all-gather.5.cloned.1.call-done) | copy-start | bytes 7864324
Sparse Core Ops, SparseCore 0:
  9.5 41.7 all-gather.4
  53.6 130.5 all-gather.8
  185.7 559.5 all-gather.6
  746.6 56.4 all-gather.10
  805.8 65.7 reduce-scatter.1
where the time goes:
time: 890 us
  waiting for transfers between devices  695 us (78%)
  blocking collectives  113 us (13%)
  matrix products  53.9 us (6%)
  between operations  13.8 us (2%)
  local copies, waits for them, and re-layouts  10.4 us (1%)
    all_gather x1, waiting for transfers between devices, local(): full_panel = lax.all_gather(weight, 'row', axis=0, tiled=True)  542 us
    all_to_all x1, blocking collectives, local(): lax.all_to_all(full_rows, ('row', 'depth'), split_axis=1, concat_axis=0,...  113 us
    reduce_scatter x1, waiting for transfers between devices, local(): lax.psum_scatter(partial_value, 'col', scatter_dimension=1, tiled=True)  53.3 us
    all_gather x1, waiting for transfers between devices, local(): full_rows = lax.all_gather(tokens, 'col', axis=1, tiled=True)  41.8 us
    all_gather x1, waiting for transfers between devices, local(): new_weight = lax.all_gather(shard_weight, 'depth', axis=0, tiled=True)  38.1 us
    dot_general x1, matrix products, local(): lax.dot_general(cotangent, full_panel, (((1,), (1,)), ((), ())), preferre...  19.8 us
    dot_general x1, matrix products, local(): lax.dot_general(token_slab, lax.all_gather(cotangent, ('row', 'depth'), a...  18.9 us
    all_gather x1, waiting for transfers between devices, local(): lax.all_gather(cotangent, ('row', 'depth'), axis=0, tiled=True)  17.8 us
  transfers between devices with their start and end apart: 5, of which 5 were waited for; matrix products, arithmetic and copies ran while one was open for 6% of the time, Pallas kernels for 0%

commit v1 on v0

--- a/solution.py
+++ b/solution.py
@@ -27,8 +27,14 @@
     token_grad = lax.psum_scatter(partial_value, "col", scatter_dimension=1, tiled=True).astype(
         jnp.bfloat16
     )
-    token_slab = lax.all_to_all(
-        full_rows, ("row", "depth"), split_axis=1, concat_axis=0, tiled=True
+    token_slab = jnp.concatenate(
+        lax.all_to_all(
+            jnp.stack(jnp.split(full_rows, lax.axis_size(("row", "depth")), axis=1)),
+            ("row", "depth"),
+            0,
+            0,
+        ),
+        axis=0,
     )
     product = lax.dot_general(
         token_slab,

time: 890 us -> 894 us (level)
  transfers between devices with their start and end apart: 5 -> 5, of which waited for: 5 -> 5; matrix products, arithmetic and copies ran while one was open for 6% -> 7% of each run, Pallas kernels for 0% -> 0%
where the time goes in v1:
time: 894 us
  waiting for transfers between devices  689 us (77%)
  blocking collectives  117 us (13%)
  matrix products  53.2 us (6%)
  local copies, waits for them, and re-layouts  17 us (2%)
  between operations  13.9 us (2%)
    all_gather x1, waiting for transfers between devices, local(): full_panel = lax.all_gather(weight, 'row', axis=0, tiled=True)  544 us
    all_to_all x1, blocking collectives, local(): lax.all_to_all(jnp.stack(jnp.split(full_rows, lax.axis_size(('row', 'dept...  117 us
    reduce_scatter x1, waiting for transfers between devices, local(): lax.psum_scatter(partial_value, 'col', scatter_dimension=1, tiled=True)  53.3 us
    all_gather x1, waiting for transfers between devices, local(): full_rows = lax.all_gather(tokens, 'col', axis=1, tiled=True)  41.8 us
    all_gather x1, waiting for transfers between devices, local(): new_weight = lax.all_gather(shard_weight, 'depth', axis=0, tiled=True)  38.1 us
    dot_general x1, matrix products, local(): lax.dot_general(cotangent, full_panel, (((1,), (1,)), ((), ())), preferre...  19.8 us
    dot_general x1, matrix products, local(): lax.dot_general(token_slab, lax.all_gather(cotangent, ('row', 'depth'), a...  18.2 us
  transfers between devices with their start and end apart: 5, of which 5 were waited for; matrix products, arithmetic and copies ran while one was open for 7% of the time, Pallas kernels for 0%

profile of v1, /device:TPU:0, one launch (start us, length us, event | category | flops | bytes accessed | tf_op | source)
XLA Modules:
  0.0 893.6 jit_solution(17808362248447207647)
XLA Ops:
  7.2 0.0 all-gather.5.cloned.1.call-start
  7.2 0.7 all-gather.5.cloned.1.call-update
  7.9 0.0 all-gather.9.cloned.1.call-start
  7.9 0.7 all-gather.9.cloned.1.call-update
  8.6 0.0 all-gather.7.cloned.1.call-start
  8.7 0.7 all-gather.7.cloned.1.call-update
  9.4 0.0 all-gather.11.cloned.1.call-start
  9.4 41.8 %all-gather.5.cloned.1.call-done = bf16[160,8192]{1,0:T(8,128)(2,1)} async-done(((bf16[160,4096]{1,0:T(8,128)(2,1)}), bf16[160,8192]{1,0:T(8,128)(2,1)}) %all-gather.5.cloned.1.call-update) | async-done | bytes 2621456 | tf_op jit(solution)/shard_map/all_gather | solution.py:19
  51.3 0.0 copy-start.1
  51.3 1.1 fusion.15
  52.4 0.9 fusion.14
  53.3 0.9 fusion.13
  54.2 0.9 fusion.12
  55.1 0.9 fusion.11
  56.1 0.9 fusion.10
  57.0 0.9 fusion.9
  57.9 0.9 fusion.8
  58.9 0.9 fusion.7
  59.8 0.0 copy-done.1
  60.0 117.0 %all_to_all.5 = bf16[16,160,512]{2,1,0:T(8,128)(2,1)} all-to-all(bf16[16,160,512]{2,1,0:T(8,128)(2,1)S(1)} %fusion), channel_id=1, replica_groups=mesh['row'=4,'col'=2,'depth'=4] {'row','depth'}, dimensions={0} | all-to-all | bytes 5242880 | tf_op jit(solution)/shard_map/all_to_all | solution.py:31
  177.0 10.4 %all-gather.9.cloned.1.call-done = bf16[2560,2048]{1,0:T(8,128)(2,1)} async-done(((bf16[160,2048]{1,0:T(8,128)(2,1)}), bf16[2560,2048]{1,0:T(8,128)(2,1)}) %all-gather.9.cloned.1.call-update) | async-done | bytes 10485776 | tf_op jit(solution)/shard_map/all_gather | solution.py:41
  187.4 18.2 %fusion.16 = (bf16[512,2048]{1,0:T(8,128)(2,1)}, f32[512,2048]{1,0:T(8,128)}, f32[512,2048]{1,0:T(8,128)}, f32[512,2048]{1,0:T(8,128)}) fusion(f32[512,2048]{1,0:T(8,128)} %param.9, f32[512,2048]{1,0:T(8,128)} %param.10, f32[512,2048]{1,0:T(8,128)} %param.11, bf16[2560,512]{1,0:T(8,128)(2,1)} %bitcast.71, bf16[2560,2048]{1,0:T(8,128)(2,1)} %all-gather.9.cloned.1.call-done), kind=kOutput, calls=%fused_computation.36 | convolution fusion | flops 5386534912 | bytes 40370176 | tf_op jit(solution)/shard_map/dot_general | solution.py:39
  205.6 0.0 copy-start
  205.6 0.0 all-gather.11.cloned.1.call-update
  205.6 0.0 reduce-scatter.2.cloned.1.call-start
  205.7 543.6 %all-gather.7.cloned.1.call-done = bf16[8192,2048]{1,0:T(8,128)(2,1)} async-done(((bf16[2048,2048]{1,0:T(8,128)(2,1)}), bf16[8192,2048]{1,0:T(8,128)(2,1)}) %all-gather.7.cloned.1.call-update) | async-done | bytes 33554448 | tf_op jit(solution)/shard_map/all_gather | solution.py:20
  749.3 0.0 copy-done
  749.3 19.8 %fusion.17 = f32[160,8192]{1,0:T(8,128)} fusion(bf16[160,2048]{1,0:T(8,128)(2,1)S(1)} %copy-done, bf16[8192,2048]{1,0:T(8,128)(2,1)} %all-gather.7.cloned.1.call-done), kind=kOutput, calls=%fused_computation.37 | convolution fusion | flops 5368709120 | bytes 39452672 | tf_op jit(solution)/shard_map/dot_general | solution.py:24
  769.1 0.0 reduce-scatter.2.cloned.1.call-update
  769.1 38.1 %all-gather.11.cloned.1.call-done = bf16[2048,2048]{1,0:T(8,128)(2,1)} async-done(((bf16[512,2048]{1,0:T(8,128)(2,1)}), bf16[2048,2048]{1,0:T(8,128)(2,1)}) %all-gather.11.cloned.1.call-update) | async-done | bytes 8388624 | tf_op jit(solution)/shard_map/all_gather | solution.py:51
  807.2 15.2 %convolution_convert_fusion = bf16[160,2048]{1,0:T(8,128)(2,1)} fusion(bf16[160,8192]{1,0:T(8,128)(2,1)S(1)} %copy-done.1, bf16[8192,2048]{1,0:T(8,128)(2,1)} %all-gather.7.cloned.1.call-done), kind=kOutput, calls=%fused_computation.3 | convolution fusion | flops 5369036800 | bytes 36831232 | tf_op jit(solution)/shard_map/dot_general | solution.py:21
  822.4 53.3 %reduce-scatter.2.cloned.1.call-done = f32[160,4096]{1,0:T(8,128)} async-done(((f32[160,8192]{1,0:T(8,128)}), f32[160,4096]{1,0:T(8,128)}) %reduce-scatter.2.cloned.1.call-update) | async-done | bytes 2621456 | tf_op jit(solution)/shard_map/reduce_scatter | solution.py:27
  875.7 3.0 convert_element_type.10
  878.6 8.4 copy.28
  (7 shorter events, 0.1 us)
Async XLA Ops:
  7.2 44.1 %all-gather.5.cloned.1.call-start = ((), (), s32[]{:S(2)}) async-start(), calls=%async_computation.2 | async-start | bytes 3932160 | tf_op jit(solution)/shard_map/all_gather | solution.py:19
  7.9 179.5 %all-gather.9.cloned.1.call-start = ((), (), s32[]{:S(2)}) async-start(), calls=%async_computation.5 | async-start | bytes 11141120 | tf_op jit(solution)/shard_map/all_gather | solution.py:41
  8.6 740.6 %all-gather.7.cloned.1.call-start = ((), (), s32[]{:S(2)}) async-start(), calls=%async_computation.3 | async-start | bytes 41943040 | tf_op jit(solution)/shard_map/all_gather | solution.py:20
  9.4 797.8 %all-gather.11.cloned.1.call-start = ((), (), s32[]{:S(2)}) async-start(), calls=%async_computation.6 | async-start | bytes 10485760 | tf_op jit(solution)/shard_map/all_gather | solution.py:51
  51.3 8.5 copy-start.1
  205.6 543.7 %copy-start = (bf16[160,2048]{1,0:T(8,128)(2,1)S(1)}, bf16[160,2048]{1,0:T(8,128)(2,1)}, u32[]{:S(2)}) copy-start(bf16[160,2048]{1,0:T(8,128)(2,1)} %param.8) | copy-start | bytes 1966084
  205.6 670.1 %reduce-scatter.2.cloned.1.call-start = ((), (), s32[]{:S(2)}) async-start(), calls=%async_computation.4 | async-start | bytes 7864320 | tf_op jit(solution)/shard_map/reduce_scatter | solution.py:27
Sparse Core Ops, SparseCore 0:
  9.5 41.7 all-gather.4
  53.6 133.7 all-gather.8
  188.9 560.2 all-gather.6
  750.7 56.4 all-gather.10
  809.9 65.7 reduce-scatter.1
